TPU v7x, 256 devices: a whole 4x4x8 slice. The times are simulated.
256 devices in a mesh: ep: 64 (over y, z, core), fs: 4 (over x).
Axes of the slice: x: 4, y: 4, z: 8, core: 2. Of those that a mesh axis runs over, the one named last changes fastest.
Arguments:
- tokens: bfloat16 [8192, 4096], P('ep', 'fs'), may hold values from -6 to 6
- grad_out: bfloat16 [8192, 4096], P('ep', 'fs'), may hold values from -6 to 6
- gate_weight: bfloat16 [4, 14336, 4096], P('fs', 'ep'), may hold values from -0.09375 to 0.09375
- up_weight: bfloat16 [4, 14336, 4096], P('fs', 'ep'), may hold values from -0.09375 to 0.09375
- down_weight: bfloat16 [4, 14336, 4096], P('fs', 'ep'), may hold values from -0.046875 to 0.046875
- gate_values: float32 [4, 256], P('fs'), may hold values from 0.25 to 1
- chosen: int32 [4, 256], replicated, may hold values from 0 to 8191, as said below
- counts: int32 [4], replicated, may hold values from 128 to 256, as said below
Outputs:
- gate_grad: bfloat16 [4, 14336, 4096], P('fs', 'ep')
- up_grad: bfloat16 [4, 14336, 4096], P('fs', 'ep')
- down_grad: bfloat16 [4, 14336, 4096], P('fs', 'ep')
- token_grad: bfloat16 [8192, 4096], P('ep', 'fs')
- score_grad: float32 [4, 256], P('fs')
Inputs may be any that keep to these rules, and one draw needn't show every extreme that they name: `chosen`: the 256 entries of one row are distinct tokens; only the first counts[e] entries of row e are live, the others are padding to be ignored. Among the live entries of one expert at most 6 lie in one aligned block of 128 tokens (the tokens of one index of ep), and in every draw every expert has exactly 6 live entries in some block. `counts`: some expert has all 256 entries live in every draw.
All inputs are finite; a program needn't handle non-finite values.
Results may differ from a plain program's by a relative error of at most 0.0057.
Values may be sent and summed in bfloat16 or wider, within the bound.
No kernel may reach another device: no remote copies, remote signals or barrier semaphores. Data moves between devices by JAX's collectives and lax.ppermute only.
A program may use at most 128 MiB of HBM per device.

v0:
```python
import jax
import jax.numpy as jnp
from jax import lax
from jax.sharding import PartitionSpec as P

SLOTS = 6


def row_products(x_rows, dy_rows, gate_rows, gate_w, up_w, down_w):
    pre_gate = jnp.einsum("rd,hd->rh", x_rows, gate_w, preferred_element_type=jnp.float32)
    pre_up = jnp.einsum("rd,hd->rh", x_rows, up_w, preferred_element_type=jnp.float32)
    sigmoid_val = jax.nn.sigmoid(pre_gate)
    swished = pre_gate * sigmoid_val
    active = (swished * pre_up).astype(jnp.bfloat16)
    probes = jnp.einsum("rd,hd->rh", dy_rows, down_w, preferred_element_type=jnp.float32)
    score_term = jnp.sum(active.astype(jnp.float32) * probes, axis=1)
    weighted = (gate_rows[:, None] * dy_rows.astype(jnp.float32)).astype(jnp.bfloat16)
    d_active = gate_rows[:, None] * probes
    d_gate = (d_active * pre_up * sigmoid_val * (1.0 + pre_gate * (1.0 - sigmoid_val))).astype(
        jnp.bfloat16
    )
    d_up = (d_active * swished).astype(jnp.bfloat16)
    return (active, weighted, d_gate, d_up, score_term)


def weight_grads(stored):
    x_store, weighted_store, active_store, gate_store, up_store = (
        stored[0],
        stored[1],
        stored[2],
        stored[3],
        stored[4],
    )
    grad_g = jnp.einsum("rh,rd->hd", gate_store, x_store, preferred_element_type=jnp.float32)
    grad_u = jnp.einsum("rh,rd->hd", up_store, x_store, preferred_element_type=jnp.float32)
    grad_d = jnp.einsum(
        "rh,rd->hd", active_store, weighted_store, preferred_element_type=jnp.float32
    )
    return (grad_g, grad_u, grad_d)


def input_rows(stored_gate, stored_up, gate_w, up_w):

    def term_rows(row_start, row_count):
        return jnp.dot(stored_gate, gate_w, preferred_element_type=jnp.float32) + jnp.dot(
            stored_up, up_w, preferred_element_type=jnp.float32
        )

    return term_rows


def on_device(tokens, grad_out, gate_weight, up_weight, down_weight, gate_values, chosen, counts):
    ep_count = lax.axis_size("ep")
    ep_index = lax.axis_index("ep")
    fs_index = lax.axis_index("fs")
    tok_rows = tokens.shape[0]
    quarter = tokens.shape[1]
    experts_here = chosen.shape[0]
    total_slots = ep_count * SLOTS
    live = lax.broadcasted_iota(jnp.int32, chosen.shape, 1) < counts[:, None]
    shard_of = chosen // tok_rows
    block_iota = lax.broadcasted_iota(jnp.int32, (1, 1, ep_count), 2)
    one_hot = ((shard_of[:, :, None] == block_iota) & live[:, :, None]).astype(jnp.int32)
    ranks = jnp.sum((jnp.cumsum(one_hot, axis=1) - one_hot) * one_hot, axis=2)
    slot_pos = jnp.where(live, shard_of * SLOTS + ranks, total_slots)
    expert_ids = lax.broadcasted_iota(jnp.int32, chosen.shape, 0)
    slot_token = (
        jnp.full((experts_here, total_slots), -1, jnp.int32)
        .at[expert_ids, slot_pos]
        .set(chosen, mode="drop")
    )
    own_slots = lax.dynamic_slice_in_dim(slot_token, ep_index * SLOTS, SLOTS, 1)
    has_row = own_slots >= 0
    local_rows = jnp.where(has_row, own_slots - ep_index * tok_rows, 0)
    zero_val = jnp.zeros((), tokens.dtype)
    picked_x = jnp.where(has_row[:, :, None], tokens[local_rows], zero_val)
    picked_dy = jnp.where(has_row[:, :, None], grad_out[local_rows], zero_val)
    own_pos = lax.dynamic_index_in_dim(slot_pos, fs_index, 0, keepdims=False)
    own_live = lax.dynamic_index_in_dim(live, fs_index, 0, keepdims=False)
    slot_gate = jnp.zeros((total_slots,), jnp.float32).at[own_pos].set(gate_values[0], mode="drop")
    gate_w = gate_weight[0]
    up_w = up_weight[0]
    down_w = down_weight[0]
    gathered_x, gathered_dy = (
        lax.all_gather(picked_x, "ep", axis=1, tiled=True),
        lax.all_gather(picked_dy, "ep", axis=1, tiled=True),
    )
    whole_x, whole_dy = (
        lax.all_to_all(gathered_x, "fs", split_axis=0, concat_axis=2, tiled=True),
        lax.all_to_all(gathered_dy, "fs", split_axis=0, concat_axis=2, tiled=True),
    )
    x_rows = whole_x[0]
    dy_rows = whole_dy[0]
    active, weighted, d_gate, d_up, score_term = row_products(
        x_rows, dy_rows, slot_gate, gate_w, up_w, down_w
    )
    stored = (x_rows, weighted, active, d_gate, d_up, score_term)
    term_rows = input_rows(stored[3], stored[4], gate_w, up_w)
    partial_rows = term_rows(0, total_slots)
    spread = lax.all_to_all(partial_rows[None], "fs", split_axis=2, concat_axis=0, tiled=True)
    grad_g, grad_u, grad_d = weight_grads(stored)
    returned = lax.psum_scatter(spread, "ep", scatter_dimension=1, tiled=True)
    score_sum = lax.psum(stored[5], "ep")
    safe_pos = jnp.minimum(own_pos, total_slots - 1)
    score_grad = jnp.where(own_live, score_sum[safe_pos], 0.0)[None]
    targets = jnp.where(has_row, local_rows, tok_rows).reshape(-1)
    token_sum = (
        jnp.zeros((tok_rows, quarter), jnp.float32)
        .at[targets]
        .add(returned.reshape(-1, quarter), mode="drop")
    )
    token_grad = token_sum.astype(jnp.bfloat16)
    return (
        grad_g.astype(jnp.bfloat16)[None],
        grad_u.astype(jnp.bfloat16)[None],
        grad_d.astype(jnp.bfloat16)[None],
        token_grad,
        score_grad,
    )


def solution(mesh):
    return jax.shard_map(
        on_device,
        mesh=mesh,
        in_specs=(
            P("ep", "fs"),
            P("ep", "fs"),
            P("fs", "ep", None),
            P("fs", "ep", None),
            P("fs", "ep", None),
            P("fs", None),
            P(),
            P(),
        ),
        out_specs=(
            P("fs", "ep", None),
            P("fs", "ep", None),
            P("fs", "ep", None),
            P("ep", "fs"),
            P("fs", None),
        ),
        check_vma=False,
    )
```

profile of v0, /device:TPU:2, one launch (start us, length us, event | category | flops | bytes accessed | tf_op | source)
XLA Modules:
  0.0 556.3 jit_solution(6767352351725591109)
XLA Ops:
  10.3 2.4 reduce-window.6
  15.4 4.3 scatter_custom_fusion.2
  20.0 1.6 gather_fusion.1
  21.6 1.6 gather_fusion
  24.8 80.4 %all-gather.5.cloned.1.call-done = bf16[4,384,1024]{2,0,1:T(4,128)(2,1)} async-done(((bf16[4,6,1024]{2,0,1:T(4,128)(2,1)}), bf16[4,384,1024]{2,0,1:T(4,128)(2,1)}) %all-gather.5.cloned.1.call-update) | async-done | bytes 3145744 | tf_op jit(solution)/shard_map/all_gather | solution.py:85
  105.2 6.3 %copy.26 = bf16[4,384,1024]{1,2,0:T(8,128)(2,1)} copy(bf16[4,384,1024]{2,0,1:T(4,128)(2,1)} %all-gather.5.cloned.1.call-done) | data formatting | bytes 6291456 | tf_op jit(solution)/shard_map/all_gather | solution.py:85
  111.5 5.2 all-to-all-start.1
  116.7 67.2 %all-gather.3.cloned.1.call-done = bf16[4,384,1024]{2,0,1:T(4,128)(2,1)} async-done(((bf16[4,6,1024]{2,0,1:T(4,128)(2,1)}), bf16[4,384,1024]{2,0,1:T(4,128)(2,1)}) %all-gather.3.cloned.1.call-update) | async-done | bytes 3145744 | tf_op jit(solution)/shard_map/all_gather | solution.py:86
  184.0 6.3 %copy.24 = bf16[4,384,1024]{1,2,0:T(8,128)(2,1)} copy(bf16[4,384,1024]{2,0,1:T(4,128)(2,1)} %all-gather.3.cloned.1.call-done) | data formatting | bytes 6291456 | tf_op jit(solution)/shard_map/all_gather | solution.py:86
  190.2 5.2 all-to-all-start
  197.0 3.6 fusion.9
  200.6 3.0 fusion.6
  203.6 28.7 %all-to-all-done = bf16[4,384,1024]{1,2,0:T(8,128)(2,1)} async-done(((bf16[4,384,1024]{1,2,0:T(8,128)(2,1)}), bf16[4,384,1024]{1,2,0:T(8,128)(2,1)}, u32[]{:S(2)}, u32[]{:S(2)}) %all-to-all-start) | async-done | bytes 3145760 | tf_op jit(solution)/shard_map/all_to_all | solution.py:90
  232.3 3.7 multiply_reduce_fusion
  237.5 3.7 add_bitcast_fusion
  241.2 14.8 %copy.27 = f32[1,384,4096]{1,0,2:T(1,128)} copy(f32[1,384,4096]{2,1,0:T(8,128)} %add_bitcast_fusion) | data formatting | bytes 12582912 | tf_op jit(solution)/shard_map/broadcast_in_dim | solution.py:100
  255.9 77.8 %all_to_all.48 = f32[1,384,4096]{1,0,2:T(1,128)} all-to-all(f32[1,384,4096]{1,0,2:T(1,128)} %copy.27), channel_id=1, replica_groups=mesh['ep'=64,'fs'=4] {'fs'}, dimensions={2} | all-to-all | bytes 12582912 | tf_op jit(solution)/shard_map/all_to_all | solution.py:100
  333.7 15.9 %copy.28 = f32[1,384,4,1024]{3,2,1,0:T(4,128)} copy(f32[1,384,4,1024]{1,0,3,2:T(1,128)} %bitcast.91) | data formatting | bytes 12582912 | tf_op jit(solution)/shard_map/all_to_all | solution.py:100
  351.6 125.2 %psum.7 = f32[384]{0:T(512)S(1)} all-reduce(f32[384]{0:T(512)S(1)} %get-tuple-element.5), channel_id=1, replica_groups=mesh['ep'=64,'fs'=4] {'ep'}, use_global_device_ids=true, to_apply=%region_8.9 | all-reduce | flops 384 | bytes 3072 | tf_op jit(solution)/shard_map/psum | solution.py:103
  476.7 1.9 gather_fusion.2
  479.3 4.4 fusion
  483.7 4.4 fusion.1
  488.0 4.6 fusion.2
  492.6 54.5 %all-reduce.3.cloned.1.call-done = f32[4,384,1024]{2,0,1:T(4,128)} async-done(((f32[4,384,1024]{2,0,1:T(4,128)}), f32[4,384,1024]{2,0,1:T(4,128)}) %all-reduce.3.cloned.1.call-update) | async-done | bytes 6291472
  (57 shorter events, 15.1 us)
Async XLA Ops:
  7.2 193.4 %copy-start = (bf16[1,224,4096]{2,1,0:T(8,128)(2,1)S(1)}, bf16[1,224,4096]{2,1,0:T(8,128)(2,1)}, u32[]{:S(2)}) copy-start(bf16[1,224,4096]{2,1,0:T(8,128)(2,1)} %param.10) | copy-start | bytes 5505028
  7.2 98.0 %all-gather.5.cloned.1.call-start = ((), (), s32[]{:S(2)}) async-start(), calls=%async_computation.4 | async-start | bytes 3194880 | tf_op jit(solution)/shard_map/all_gather | solution.py:85
  24.1 159.9 %all-gather.3.cloned.1.call-start = ((), (), s32[]{:S(2)}) async-start(), calls=%async_computation.3 | async-start | bytes 3194880 | tf_op jit(solution)/shard_map/all_gather | solution.py:86
  111.5 78.7 %all-to-all-start.1 = ((bf16[4,384,1024]{1,2,0:T(8,128)(2,1)}), bf16[4,384,1024]{1,2,0:T(8,128)(2,1)}, u32[]{:S(2)}, u32[]{:S(2)}) async-start(bf16[4,384,1024]{1,2,0:T(8,128)(2,1)} %copy.26), calls=%async_computation.1 | async-start | bytes 6291456 | tf_op jit(solution)/shard_map/all_to_all | solution.py:89
  190.2 42.1 %all-to-all-start = ((bf16[4,384,1024]{1,2,0:T(8,128)(2,1)}), bf16[4,384,1024]{1,2,0:T(8,128)(2,1)}, u32[]{:S(2)}, u32[]{:S(2)}) async-start(bf16[4,384,1024]{1,2,0:T(8,128)(2,1)} %copy.24), calls=%async_computation | async-start | bytes 6291456 | tf_op jit(solution)/shard_map/all_to_all | solution.py:90
  195.4 351.7 %all-reduce.3.cloned.1.call-start = ((), (), s32[]{:S(2)}) async-start(), calls=%async_computation.5 | async-start | bytes 12582912
  236.0 1.5 copy-start.2
  349.6 0.7 copy-start.3
  488.0 61.7 %copy-start.1 = (bf16[1,224,4096]{2,1,0:T(8,128)(2,1)S(1)}, bf16[1,224,4096]{2,1,0:T(8,128)(2,1)}, u32[]{:S(2)}) copy-start(bf16[1,224,4096]{2,1,0:T(8,128)(2,1)} %param.10) | copy-start | bytes 5505028
Sparse Core Ops, SparseCore 0:
  24.2 80.9 all-gather.4
  108.5 75.3 all-gather.2
  349.8 197.2 all-reduce.2
where the time goes:
time: 558 us; the launch traced here: 556 us
  waiting for transfers between devices  231 us (41%)
  blocking collectives  203 us (36%)
  local copies, waits for them, and re-layouts  59.5 us (11%)
  matrix products  28.3 us (5%)
  between operations  14.6 us (3%)
  starting transfers between devices  10.5 us (2%)
  other arithmetic  9.64 us (2%)
    psum x1, blocking collectives, on_device(): score_sum = lax.psum(stored[5], 'ep')  125 us
    all_gather x1, waiting for transfers between devices, on_device(): lax.all_gather(picked_x, 'ep', axis=1, tiled=True)  80.4 us
    all_to_all x1, blocking collectives, on_device(): lax.all_to_all(partial_rows[None], 'fs', split_axis=2, concat_axis=0, til...  77.8 us
    all_gather x1, waiting for transfers between devices, on_device(): lax.all_gather(picked_dy, 'ep', axis=1, tiled=True)  67.2 us
    unnamed x4, waiting for transfers between devices  54.6 us
    all_to_all x1, waiting for transfers between devices, on_device(): lax.all_to_all(gathered_dy, 'fs', split_axis=0, concat_axis=2, tiled=True)  28.7 us
    all_to_all x1, local copies, waits for them, and re-layouts, on_device(): lax.all_to_all(partial_rows[None], 'fs', split_axis=2, concat_axis=0, til...  15.9 us
    broadcast_in_dim x1, local copies, waits for them, and re-layouts, on_device(): partial_rows[None]  14.8 us
  transfers between devices with their start and end apart: 5, of which 4 were waited for; matrix products, arithmetic and copies ran while one was open for 7% of the time, Pallas kernels for 0%

commit v1 on v0

--- a/solution.py
+++ b/solution.py
@@ -97,7 +97,12 @@
     stored = (x_rows, weighted, active, d_gate, d_up, score_term)
     term_rows = input_rows(stored[3], stored[4], gate_w, up_w)
     partial_rows = term_rows(0, total_slots)
-    spread = lax.all_to_all(partial_rows[None], "fs", split_axis=2, concat_axis=0, tiled=True)
+    spread = jnp.concatenate(
+        lax.all_to_all(
+            jnp.stack(jnp.split(partial_rows[None], lax.axis_size("fs"), axis=2)), "fs", 0, 0
+        ),
+        axis=0,
+    )
     grad_g, grad_u, grad_d = weight_grads(stored)
     returned = lax.psum_scatter(spread, "ep", scatter_dimension=1, tiled=True)
     score_sum = lax.psum(stored[5], "ep")

time: 558 us -> 528 us (0.946)
  local copies, waits for them, and re-layouts: 59.5 us -> 36.5 us
    all_to_all x1 -> x0, local copies, waits for them, and re-layouts: 15.9 us -> none  [on_device(): lax.all_to_all(partial_rows[None], 'fs', split_axis=2, concat_axis=0, til...]
    broadcast_in_dim x1 -> x0, local copies, waits for them, and re-layouts: 14.8 us -> none  [on_device(): partial_rows[None]]
    reshape x0 -> x1, local copies, waits for them, and re-layouts: none -> 6.7 us  [on_device(): jnp.concatenate(lax.all_to_all(jnp.stack(jnp.split(partial_rows[None], la...]
where the time goes in v1:
time: 528 us; the launch traced here: 527 us
  waiting for transfers between devices  231 us (44%)
  blocking collectives  199 us (38%)
  local copies, waits for them, and re-layouts  36.5 us (7%)
  matrix products  25.6 us (5%)
  between operations  14.6 us (3%)
  starting transfers between devices  10.5 us (2%)
  other arithmetic  10.4 us (2%)
    psum x1, blocking collectives, on_device(): score_sum = lax.psum(stored[5], 'ep')  125 us
    all_gather x1, waiting for transfers between devices, on_device(): lax.all_gather(picked_x, 'ep', axis=1, tiled=True)  80.4 us
    all_to_all x1, blocking collectives, on_device(): lax.all_to_all(jnp.stack(jnp.split(partial_rows[None], lax.axis_size('fs'...  73.7 us
    all_gather x1, waiting for transfers between devices, on_device(): lax.all_gather(picked_dy, 'ep', axis=1, tiled=True)  67.2 us
    unnamed x4, waiting for transfers between devices  54.6 us
    all_to_all x1, waiting for transfers between devices, on_device(): lax.all_to_all(gathered_dy, 'fs', split_axis=0, concat_axis=2, tiled=True)  28.7 us
  transfers between devices with their start and end apart: 5, of which 4 were waited for; matrix products, arithmetic and copies ran while one was open for 7% of the time, Pallas kernels for 0%

profile of v1, /device:TPU:2, one launch (start us, length us, event | category | flops | bytes accessed | tf_op | source)
XLA Modules:
  0.0 527.2 jit_solution(459771422427117317)
XLA Ops:
  10.3 2.4 reduce-window.6
  15.4 4.3 scatter_custom_fusion.2
  20.0 1.6 gather_fusion.1
  21.6 1.6 gather_fusion
  24.8 80.4 %all-gather.5.cloned.1.call-done = bf16[4,384,1024]{2,0,1:T(4,128)(2,1)} async-done(((bf16[4,6,1024]{2,0,1:T(4,128)(2,1)}), bf16[4,384,1024]{2,0,1:T(4,128)(2,1)}) %all-gather.5.cloned.1.call-update) | async-done | bytes 3145744 | tf_op jit(solution)/shard_map/all_gather | solution.py:85
  105.2 6.3 %copy.24 = bf16[4,384,1024]{1,2,0:T(8,128)(2,1)} copy(bf16[4,384,1024]{2,0,1:T(4,128)(2,1)} %all-gather.5.cloned.1.call-done) | data formatting | bytes 6291456 | tf_op jit(solution)/shard_map/all_gather | solution.py:85
  111.5 5.2 all-to-all-start.1
  116.7 67.2 %all-gather.3.cloned.1.call-done = bf16[4,384,1024]{2,0,1:T(4,128)(2,1)} async-done(((bf16[4,6,1024]{2,0,1:T(4,128)(2,1)}), bf16[4,384,1024]{2,0,1:T(4,128)(2,1)}) %all-gather.3.cloned.1.call-update) | async-done | bytes 3145744 | tf_op jit(solution)/shard_map/all_gather | solution.py:86
  184.0 6.3 %copy.22 = bf16[4,384,1024]{1,2,0:T(8,128)(2,1)} copy(bf16[4,384,1024]{2,0,1:T(4,128)(2,1)} %all-gather.3.cloned.1.call-done) | data formatting | bytes 6291456 | tf_op jit(solution)/shard_map/all_gather | solution.py:86
  190.2 5.2 all-to-all-start
  195.4 1.6 scatter_custom_fusion
  197.0 3.6 fusion.9
  200.6 3.0 fusion.6
  203.6 28.7 %all-to-all-done = bf16[4,384,1024]{1,2,0:T(8,128)(2,1)} async-done(((bf16[4,384,1024]{1,2,0:T(8,128)(2,1)}), bf16[4,384,1024]{1,2,0:T(8,128)(2,1)}, u32[]{:S(2)}, u32[]{:S(2)}) %all-to-all-start) | async-done | bytes 3145760 | tf_op jit(solution)/shard_map/all_to_all | solution.py:90
  232.3 3.7 multiply_reduce_fusion
  237.5 1.0 add_bitcast_fusion
  240.3 73.7 %all_to_all.35 = f32[4,1,384,1024]{3,2,1,0:T(8,128)S(1)} all-to-all(f32[4,1,384,1024]{3,2,1,0:T(8,128)S(1)} %pad_maximum_fusion), channel_id=1, replica_groups=mesh['ep'=64,'fs'=4] {'fs'}, dimensions={0} | all-to-all | bytes 12582912 | tf_op jit(solution)/shard_map/all_to_all | solution.py:101
  314.0 6.7 %copy.25 = f32[4,384,1024]{2,0,1:T(4,128)} copy(f32[4,384,1024]{2,1,0:T(8,128)S(1)} %bitcast.95) | data formatting | bytes 12582912 | tf_op jit(solution)/shard_map/reshape | solution.py:100
  322.6 125.0 %psum.7 = f32[384]{0:T(512)S(1)} all-reduce(f32[384]{0:T(512)S(1)} %get-tuple-element.5), channel_id=1, replica_groups=mesh['ep'=64,'fs'=4] {'ep'}, use_global_device_ids=true, to_apply=%region_8.9 | all-reduce | flops 384 | bytes 3072 | tf_op jit(solution)/shard_map/psum | solution.py:108
  447.6 1.9 gather_fusion.2
  450.2 4.4 fusion
  454.6 4.4 fusion.1
  458.9 4.6 fusion.2
  463.5 54.5 %all-reduce.3.cloned.1.call-done = f32[4,384,1024]{2,0,1:T(4,128)} async-done(((f32[4,384,1024]{2,0,1:T(4,128)}), f32[4,384,1024]{2,0,1:T(4,128)}) %all-reduce.3.cloned.1.call-update) | async-done | bytes 6291472
  (58 shorter events, 15.3 us)
Async XLA Ops:
  7.2 193.4 %copy-start = (bf16[1,224,4096]{2,1,0:T(8,128)(2,1)S(1)}, bf16[1,224,4096]{2,1,0:T(8,128)(2,1)}, u32[]{:S(2)}) copy-start(bf16[1,224,4096]{2,1,0:T(8,128)(2,1)} %param.10) | copy-start | bytes 5505028
  7.2 98.0 %all-gather.5.cloned.1.call-start = ((), (), s32[]{:S(2)}) async-start(), calls=%async_computation.4 | async-start | bytes 3194880 | tf_op jit(solution)/shard_map/all_gather | solution.py:85
  24.1 159.9 %all-gather.3.cloned.1.call-start = ((), (), s32[]{:S(2)}) async-start(), calls=%async_computation.3 | async-start | bytes 3194880 | tf_op jit(solution)/shard_map/all_gather | solution.py:86
  111.5 78.7 %all-to-all-start.1 = ((bf16[4,384,1024]{1,2,0:T(8,128)(2,1)}), bf16[4,384,1024]{1,2,0:T(8,128)(2,1)}, u32[]{:S(2)}, u32[]{:S(2)}) async-start(bf16[4,384,1024]{1,2,0:T(8,128)(2,1)} %copy.24), calls=%async_computation.1 | async-start | bytes 6291456 | tf_op jit(solution)/shard_map/all_to_all | solution.py:89
  190.2 42.1 %all-to-all-start = ((bf16[4,384,1024]{1,2,0:T(8,128)(2,1)}), bf16[4,384,1024]{1,2,0:T(8,128)(2,1)}, u32[]{:S(2)}, u32[]{:S(2)}) async-start(bf16[4,384,1024]{1,2,0:T(8,128)(2,1)} %copy.22), calls=%async_computation | async-start | bytes 6291456 | tf_op jit(solution)/shard_map/all_to_all | solution.py:90
  195.4 322.6 %all-reduce.3.cloned.1.call-start = ((), (), s32[]{:S(2)}) async-start(), calls=%async_computation.5 | async-start | bytes 12582912
  236.0 1.5 copy-start.2
  320.7 0.7 copy-start.3
  458.9 61.7 %copy-start.1 = (bf16[1,224,4096]{2,1,0:T(8,128)(2,1)S(1)}, bf16[1,224,4096]{2,1,0:T(8,128)(2,1)}, u32[]{:S(2)}) copy-start(bf16[1,224,4096]{2,1,0:T(8,128)(2,1)} %param.10) | copy-start | bytes 5505028
Sparse Core Ops, SparseCore 0:
  24.2 80.9 all-gather.4
  108.5 75.3 all-gather.2
  320.8 197.1 all-reduce.2
